TPU v7x, 256 devices: a whole 4x4x8 slice. The times are simulated.
256 devices in a mesh: px: 16 (over y, x), py: 16 (over z, core).
Axes of the slice: x: 4, y: 4, z: 8, core: 2. Of those that a mesh axis runs over, the one named last changes fastest.
Arguments:
- start_field: float32 [128, 256, 512], P('px', 'py'), may hold values from -1.7 to 1.7
- known: float32 [8, 128, 256, 512], P(None, 'px', 'py'), may hold values from -1 to 1
Outputs:
- solution_field: float32 [128, 256, 512], P('px', 'py')
- residual: float32 [128, 256, 512], P('px', 'py')
All inputs are finite; a program needn't handle non-finite values.
Results may differ from a plain program's by a relative error of at most 0.01.
Values sent between devices are 32-bit elements; how exact they have to be, the bound alone decides.
No kernel may reach another device: no remote copies, remote signals or barrier semaphores. Data moves between devices by JAX's collectives and lax.ppermute only.
A program may use at most 64 MiB of HBM per device.

v0:
```python
import jax
import jax.numpy as jnp
from jax import lax
from jax.sharding import PartitionSpec as P

NEWTON = 2
ITERS = 3
DIFFUSION = 0.5
SHIFT = 4.0
EPS = 1e-06


def extended(cells, sides, width):
    for axis, dim in sides:
        count = lax.axis_size(axis)
        ends = count - 1
        head = lax.slice_in_dim(cells, 0, width, axis=dim)
        tail = lax.slice_in_dim(cells, cells.shape[dim] - width, cells.shape[dim], axis=dim)
        cells = jnp.concatenate(
            [
                lax.ppermute(tail, axis, [(i, (i + 1) % count) for i in range(ends)]),
                cells,
                lax.ppermute(head, axis, [((i + 1) % count, i) for i in range(ends)]),
            ],
            axis=dim,
        )
    return cells


def laplace(field):
    padded = extended(field, (("px", 0), ("py", 1)), 1)
    zero = jnp.zeros_like(field[:, :, :1])
    upper = jnp.concatenate([field[:, :, 1:], zero], axis=2)
    lower = jnp.concatenate([zero, field[:, :, :-1]], axis=2)
    beside = padded[2:, 1:-1, :] + padded[:-2, 1:-1, :]
    beside = beside + padded[1:-1, 2:, :] + padded[1:-1, :-2, :]
    return beside + upper + lower - 6.0 * field


def allen_cahn(field, lap):
    return DIFFUSION * lap + field - field * field * field


def solve_small(hess, beta):
    normal = jnp.sum(hess[:, :, None] * hess[:, None, :], axis=0)
    target = beta * hess[0]
    lower = jnp.linalg.cholesky(normal)
    count = normal.shape[0]
    forward = []
    for i in range(count):
        acc = target[i]
        for j in range(i):
            acc = acc - lower[i, j] * forward[j]
        forward.append(acc / lower[i, i])
    back = [None] * count
    for i in reversed(range(count)):
        acc = forward[i]
        for j in range(i + 1, count):
            acc = acc - lower[j, i] * back[j]
        back[i] = acc / lower[i, i]
    return jnp.stack(back)


def local(start_field, known):
    cells = float(
        start_field.shape[0]
        * lax.axis_size("px")
        * start_field.shape[1]
        * lax.axis_size("py")
        * start_field.shape[2]
    )
    field = start_field
    lap_field = laplace(field)
    for step in range(NEWTON):
        force = allen_cahn(field, lap_field)
        diffs = field[None] - known
        dist_local = jnp.sum(diffs * diffs, axis=(1, 2, 3))
        first_sum, force_sq = lax.psum((dist_local, jnp.sum(force * force)), ("px", "py"))
        beta = jnp.sqrt(force_sq + EPS)
        basis = [-force / beta]
        lap_basis = []
        jac_diag = 1.0 - 3.0 * field * field
        hess = jnp.zeros((ITERS + 1, ITERS), jnp.float32)
        for k in range(ITERS):
            lap_vec = laplace(basis[k])
            lap_basis.append(lap_vec)
            image = DIFFUSION * lap_vec + jac_diag * basis[k]
            heights_local = jnp.stack([jnp.sum(vec * image) for vec in basis])
            summed = lax.psum(heights_local, ("px", "py"))
            rest = image
            for j in range(k + 1):
                rest = rest - summed[j] * basis[j]
            height = jnp.sqrt(lax.psum(jnp.sum(rest * rest), ("px", "py")) + EPS)
            hess = hess.at[: k + 1, k].set(summed).at[k + 1, k].set(height)
            if k < ITERS - 1:
                basis.append(rest / height)
        coeffs = solve_small(hess, beta)
        delta = coeffs[0] * basis[0]
        for j in range(1, ITERS):
            delta = delta + coeffs[j] * basis[j]
        inner = lax.psum(jnp.sum(diffs * delta[None], axis=(1, 2, 3)), ("px", "py"))
        mean_dist = first_sum / cells + EPS
        weight = 1.0 / mean_dist + SHIFT
        total = jnp.sum(2.0 * inner / (cells * mean_dist * mean_dist * weight))
        scale = 1.0 / (1.0 + jnp.abs(total))
        field = field + scale * delta
        lap_field = laplace(field)
    return (field, allen_cahn(field, lap_field))


def solution(mesh):
    placed = (P("px", "py", None), P(None, "px", "py", None))
    return jax.shard_map(
        local,
        mesh=mesh,
        in_specs=placed,
        out_specs=(P("px", "py", None), P("px", "py", None)),
        check_vma=False,
    )
```

profile of v0, /device:TPU:38, one launch (start us, length us, event | category | flops | bytes accessed | tf_op | source)
XLA Modules:
  0.0 1435.6 jit_solution(6165251050151356504)
XLA Ops:
  1.5 2.7 collective-permute-start
  4.2 5.2 collective-permute-start.1
  19.9 80.0 %psum.126 = f32[]{:T(128)} all-reduce(f32[]{:T(128)} %get-tuple-element.179), channel_id=1, replica_groups=mesh['px'=16,'py'=16] {'px','py'}, use_global_device_ids=true, to_apply=%region_1.0 | all-reduce | flops 1 | bytes 8 | tf_op jit(solution)/shard_map/psum | solution.py:78
  100.6 3.4 collective-permute-start.5
  104.0 2.5 collective-permute-start.4
  107.2 4.7 collective-permute-done.4
  116.5 2.5 collective-permute-done.7
  119.8 73.3 %psum.127 = f32[1]{0:T(128)} all-reduce(f32[1]{0:T(128)} %bitcast), channel_id=1, replica_groups=mesh['px'=16,'py'=16] {'px','py'}, use_global_device_ids=true, to_apply=%region_3.0 | all-reduce | flops 1 | bytes 8 | tf_op jit(solution)/shard_map/psum | solution.py:89
  194.5 74.3 %psum.128 = f32[]{:T(128)} all-reduce(f32[]{:T(128)} %multiply_reduce_fusion.21), channel_id=1, replica_groups=mesh['px'=16,'py'=16] {'px','py'}, use_global_device_ids=true, to_apply=%region_5.0 | all-reduce | flops 1 | bytes 8 | tf_op jit(solution)/shard_map/psum | solution.py:93
  270.2 3.4 collective-permute-start.9
  273.6 2.5 collective-permute-start.8
  277.3 4.1 collective-permute-done.8
  291.0 73.4 %psum.129 = f32[2]{0:T(128)S(1)} all-reduce(f32[2]{0:T(128)S(1)} %pad_maximum_fusion.92), channel_id=1, replica_groups=mesh['px'=16,'py'=16] {'px','py'}, use_global_device_ids=true, to_apply=%region_9.0 | all-reduce | flops 2 | bytes 16 | tf_op jit(solution)/shard_map/psum | solution.py:89
  367.1 74.1 %psum.130 = f32[]{:T(128)} all-reduce(f32[]{:T(128)} %get-tuple-element.174), channel_id=1, replica_groups=mesh['px'=16,'py'=16] {'px','py'}, use_global_device_ids=true, to_apply=%region_11.0 | all-reduce | flops 1 | bytes 8 | tf_op jit(solution)/shard_map/psum | solution.py:93
  441.9 3.4 collective-permute-start.13
  448.6 4.6 collective-permute-done.12
  461.1 2.8 multiply_reduce_fusion.17
  466.0 75.2 %psum.131 = f32[3]{0:T(128)S(1)} all-reduce(f32[3]{0:T(128)S(1)} %pad_maximum_fusion.93), channel_id=1, replica_groups=mesh['px'=16,'py'=16] {'px','py'}, use_global_device_ids=true, to_apply=%region_16.0 | all-reduce | flops 3 | bytes 24 | tf_op jit(solution)/shard_map/psum | solution.py:89
  543.7 3.6 multiply_reduce_fusion.14
  548.8 74.0 %psum.132 = f32[]{:T(128)} all-reduce(f32[]{:T(128)} %multiply_reduce_fusion.14), channel_id=1, replica_groups=mesh['px'=16,'py'=16] {'px','py'}, use_global_device_ids=true, to_apply=%region_18.0 | all-reduce | flops 1 | bytes 8 | tf_op jit(solution)/shard_map/psum | solution.py:93
  636.7 73.7 %all-reduce.21 = (f32[8]{0:T(128)S(1)}, f32[8]{0:T(128)S(1)}) all-reduce(f32[8]{0:T(128)S(1)} %get-tuple-element.150, f32[8]{0:T(128)S(1)} %get-tuple-element.149), channel_id=1, replica_groups=mesh['px'=16,'py'=16] {'px','py'}, use_global_device_ids=true, to_apply=%region_25.27 | all-reduce | flops 16 | bytes 128 | tf_op jit(solution)/shard_map/psum | solution.py:78
  711.9 3.3 collective-permute-start.17
  715.2 2.5 collective-permute-start.16
  717.7 5.4 collective-permute-done.16
  727.6 2.5 collective-permute-done.19
  731.0 73.4 %psum.135 = f32[]{:T(128)} all-reduce(f32[]{:T(128)} %get-tuple-element.171), channel_id=1, replica_groups=mesh['px'=16,'py'=16] {'px','py'}, use_global_device_ids=true, to_apply=%region_28.0 | all-reduce | flops 1 | bytes 8 | tf_op jit(solution)/shard_map/psum | solution.py:78
  805.1 3.4 collective-permute-start.21
  808.5 2.5 collective-permute-start.20
  811.0 5.4 collective-permute-done.20
  820.9 2.5 collective-permute-done.23
  824.3 73.4 %psum.136 = f32[1]{0:T(128)} all-reduce(f32[1]{0:T(128)} %bitcast.32), channel_id=1, replica_groups=mesh['px'=16,'py'=16] {'px','py'}, use_global_device_ids=true, to_apply=%region_30.0 | all-reduce | flops 1 | bytes 8 | tf_op jit(solution)/shard_map/psum | solution.py:89
  899.0 74.1 %psum.137 = f32[]{:T(128)} all-reduce(f32[]{:T(128)} %multiply_reduce_fusion.11), channel_id=1, replica_groups=mesh['px'=16,'py'=16] {'px','py'}, use_global_device_ids=true, to_apply=%region_32.0 | all-reduce | flops 1 | bytes 8 | tf_op jit(solution)/shard_map/psum | solution.py:93
  974.5 3.4 collective-permute-start.25
  977.9 2.5 collective-permute-start.24
  980.4 5.4 collective-permute-done.24
  995.3 73.4 %psum.138 = f32[2]{0:T(128)S(1)} all-reduce(f32[2]{0:T(128)S(1)} %pad_maximum_fusion.94), channel_id=1, replica_groups=mesh['px'=16,'py'=16] {'px','py'}, use_global_device_ids=true, to_apply=%region_35.0 | all-reduce | flops 2 | bytes 16 | tf_op jit(solution)/shard_map/psum | solution.py:89
  1071.4 74.0 %psum.139 = f32[]{:T(128)} all-reduce(f32[]{:T(128)} %get-tuple-element.166), channel_id=1, replica_groups=mesh['px'=16,'py'=16] {'px','py'}, use_global_device_ids=true, to_apply=%region_37.0 | all-reduce | flops 1 | bytes 8 | tf_op jit(solution)/shard_map/psum | solution.py:93
  1146.1 3.4 collective-permute-start.29
  1152.9 4.6 collective-permute-done.28
  1166.0 2.7 multiply_reduce_fusion.7
  1170.8 75.2 %psum.140 = f32[3]{0:T(128)S(1)} all-reduce(f32[3]{0:T(128)S(1)} %pad_maximum_fusion.95), channel_id=1, replica_groups=mesh['px'=16,'py'=16] {'px','py'}, use_global_device_ids=true, to_apply=%region_41.0 | all-reduce | flops 3 | bytes 24 | tf_op jit(solution)/shard_map/psum | solution.py:89
  1248.5 3.6 multiply_reduce_fusion.4
  1253.5 74.1 %psum.141 = f32[]{:T(128)} all-reduce(f32[]{:T(128)} %multiply_reduce_fusion.4), channel_id=1, replica_groups=mesh['px'=16,'py'=16] {'px','py'}, use_global_device_ids=true, to_apply=%region_43.0 | all-reduce | flops 1 | bytes 8 | tf_op jit(solution)/shard_map/psum | solution.py:93
  1341.6 73.5 %all-reduce.20 = (f32[8]{0:T(128)S(1)}, f32[8]{0:T(128)S(1)}) all-reduce(f32[8]{0:T(128)S(1)} %get-tuple-element.148, f32[8]{0:T(128)S(1)} %get-tuple-element.147), channel_id=1, replica_groups=mesh['px'=16,'py'=16] {'px','py'}, use_global_device_ids=true, to_apply=%region_48.0 | all-reduce | flops 16 | bytes 128 | tf_op jit(solution)/shard_map/psum | solution.py:78
  1416.4 3.3 collective-permute-start.33
  1419.8 2.5 collective-permute-start.32
  1422.3 5.4 collective-permute-done.32
  1432.2 2.5 collective-permute-done.35
  (157 shorter events, 107.0 us)
Async XLA Ops:
  0.6 18.4 %copy-start = (f32[8,16,512]{2,1,0:T(8,128)S(1)}, f32[8,16,512]{2,1,0:T(8,128)}, u32[]{:S(2)}) copy-start(f32[8,16,512]{2,1,0:T(8,128)} %param.27) | copy-start | bytes 786436
  1.5 10.5 collective-permute-start
  4.2 6.8 collective-permute-start.1
  12.0 5.6 collective-permute-start.2
  14.0 5.1 collective-permute-start.3
  100.6 6.5 collective-permute-start.5
  104.0 7.9 collective-permute-start.4
  112.0 4.5 collective-permute-start.6
  113.9 5.1 collective-permute-start.7
  270.2 7.1 collective-permute-start.9
  273.6 7.9 collective-permute-start.8
  281.5 5.1 collective-permute-start.10
  283.4 5.1 collective-permute-start.11
  441.9 6.7 collective-permute-start.13
  445.3 7.9 collective-permute-start.12
  453.2 7.9 collective-permute-start.14
  455.1 6.0 collective-permute-start.15
  461.1 175.0 %copy-start.1 = (f32[8,8,16,512]{3,2,1,0:T(8,128)S(1)}, f32[8,8,16,512]{3,2,1,0:T(8,128)}, u32[]{:S(2)}) copy-start(f32[8,8,16,512]{3,2,1,0:T(8,128)} %param.28) | copy-start | bytes 6291460
  711.9 5.9 collective-permute-start.17
  715.2 7.9 collective-permute-start.16
  723.1 4.5 collective-permute-start.18
  725.0 5.1 collective-permute-start.19
  805.1 5.9 collective-permute-start.21
  808.5 7.9 collective-permute-start.20
  816.4 4.5 collective-permute-start.22
  818.3 5.1 collective-permute-start.23
  974.5 5.9 collective-permute-start.25
  977.9 7.9 collective-permute-start.24
  985.8 5.1 collective-permute-start.26
  987.8 5.1 collective-permute-start.27
  1146.1 6.7 collective-permute-start.29
  1149.5 7.9 collective-permute-start.28
  1158.1 7.9 collective-permute-start.30
  1160.0 6.0 collective-permute-start.31
  1416.4 19.2 %copy-start.2 = (f32[8,16,512]{2,1,0:T(8,128)}, f32[8,16,512]{2,1,0:T(8,128)S(1)}, u32[]{:S(2)}) copy-start(f32[8,16,512]{2,1,0:T(8,128)S(1)} %multiply_add_fusion) | copy-start | bytes 786436
  1416.4 5.9 collective-permute-start.33
  1419.8 7.9 collective-permute-start.32
  1427.7 4.5 collective-permute-start.34
  1429.6 5.1 collective-permute-start.35
where the time goes:
time: 1440 us
  blocking collectives  1190 us (83%)
  starting transfers between devices  93.6 us (6%)
  waiting for transfers between devices  55.3 us (4%)
  other arithmetic  50.1 us (3%)
  between operations  27.2 us (2%)
  local copies, waits for them, and re-layouts  20.1 us (1%)
    psum x6, blocking collectives, local(): height = jnp.sqrt(lax.psum(jnp.sum(rest * rest), ('px', 'py')) + EPS)  445 us
    psum x6, blocking collectives, local(): summed = lax.psum(heights_local, ('px', 'py'))  444 us
    psum x4, blocking collectives, local(): lax.psum((dist_local, jnp.sum(force * force)), ('px', 'py'))  301 us
    ppermute x18, starting transfers between devices, extended(): lax.ppermute(tail, axis, [(i, (i + 1) % count) for i in range(ends)])  53.6 us
    ppermute x18, starting transfers between devices, extended(): lax.ppermute(head, axis, [((i + 1) % count, i) for i in range(ends)])  40 us
    ppermute x18, waiting for transfers between devices, extended(): lax.ppermute(head, axis, [((i + 1) % count, i) for i in range(ends)])  39.6 us
  transfers between devices with their start and end apart: 36, of which 16 were waited for; matrix products, arithmetic and copies ran while one was open for 1% of the time, Pallas kernels for 0%

commit v1 on v0

--- a/solution.py
+++ b/solution.py
@@ -1,3 +1,4 @@
+import functools
 import jax
 import jax.numpy as jnp
 from jax import lax
@@ -8,6 +9,15 @@
 DIFFUSION = 0.5
 SHIFT = 4.0
 EPS = 1e-06
+
+
+def feed_panel(panel, row_axis, link_axis):
+    for dev_i in (row_axis, link_axis):
+        panel = lax.psum(panel, axis_name=dev_i)
+    return panel
+
+
+mix_spans = functools.partial(feed_panel, row_axis="px", link_axis="py")
 
 
 def extended(cells, sides, width):
@@ -86,7 +96,7 @@
             lap_basis.append(lap_vec)
             image = DIFFUSION * lap_vec + jac_diag * basis[k]
             heights_local = jnp.stack([jnp.sum(vec * image) for vec in basis])
-            summed = lax.psum(heights_local, ("px", "py"))
+            summed = mix_spans(heights_local)
             rest = image
             for j in range(k + 1):
                 rest = rest - summed[j] * basis[j]

time: 1440 us -> 1340 us (0.931)
  blocking collectives: 1190 us -> 1090 us
    psum x6 -> x12, blocking collectives: 444 us -> 303 us  [feed_panel(): panel = lax.psum(panel, axis_name=dev_i)]
    psum x6, blocking collectives: 445 us -> 488 us  [local(): height = jnp.sqrt(lax.psum(jnp.sum(rest * rest), ('px', 'py')) + EPS)]
  transfers between devices with their start and end apart: 36 -> 36, of which waited for: 16 -> 18; matrix products, arithmetic and copies ran while one was open for 1% -> 1% of each run, Pallas kernels for 0% -> 0%
where the time goes in v1:
time: 1340 us; the launch traced here: 1330 us
  blocking collectives  1090 us (81%)
  starting transfers between devices  91.7 us (7%)
  waiting for transfers between devices  64.7 us (5%)
  other arithmetic  42.9 us (3%)
  between operations  27.6 us (2%)
  local copies, waits for them, and re-layouts  18.4 us (1%)
    psum x6, blocking collectives, local(): height = jnp.sqrt(lax.psum(jnp.sum(rest * rest), ('px', 'py')) + EPS)  488 us
    psum x12, blocking collectives, feed_panel(): panel = lax.psum(panel, axis_name=dev_i)  303 us
    psum x4, blocking collectives, local(): lax.psum((dist_local, jnp.sum(force * force)), ('px', 'py'))  297 us
    ppermute x18, starting transfers between devices, extended(): lax.ppermute(tail, axis, [(i, (i + 1) % count) for i in range(ends)])  51.6 us
    ppermute x18, waiting for transfers between devices, extended(): lax.ppermute(head, axis, [((i + 1) % count, i) for i in range(ends)])  45.5 us
    ppermute x18, starting transfers between devices, extended(): lax.ppermute(head, axis, [((i + 1) % count, i) for i in range(ends)])  40.1 us
  transfers between devices with their start and end apart: 36, of which 18 were waited for; matrix products, arithmetic and copies ran while one was open for 1% of the time, Pallas kernels for 0%

profile of v1, /device:TPU:38, one launch (start us, length us, event | category | flops | bytes accessed | tf_op | source)
XLA Modules:
  0.0 1333.5 jit_solution(14833187763406653205)
XLA Ops:
  1.5 3.4 collective-permute-start.1
  8.3 4.5 collective-permute-done
  20.7 76.6 %psum.168 = f32[]{:T(128)} all-reduce(f32[]{:T(128)} %get-tuple-element.179), channel_id=1, replica_groups=mesh['px'=16,'py'=16] {'px','py'}, use_global_device_ids=true, to_apply=%region_1.0 | all-reduce | flops 1 | bytes 8 | tf_op jit(solution)/shard_map/psum | solution.py:88
  98.1 3.4 collective-permute-start.5
  104.6 4.7 collective-permute-done.4
  113.9 2.5 collective-permute-done.7
  117.2 31.0 %psum.169 = f32[1]{0:T(128)} all-reduce(f32[1]{0:T(128)} %bitcast), channel_id=1, replica_groups=mesh['px'=16,'py'=16] {'px'}, use_global_device_ids=true, to_apply=%region_3.0 | all-reduce | flops 1 | bytes 8 | tf_op jit(solution)/shard_map/psum | solution.py:16
  148.9 19.9 %psum.170 = f32[1]{0:T(128)} all-reduce(f32[1]{0:T(128)} %psum.169), channel_id=1, replica_groups=mesh['px'=16,'py'=16] {'py'}, use_global_device_ids=true, to_apply=%region_4.0 | all-reduce | flops 1 | bytes 8 | tf_op jit(solution)/shard_map/psum | solution.py:16
  170.1 81.5 %psum.171 = f32[]{:T(128)} all-reduce(f32[]{:T(128)} %multiply_reduce_fusion.21), channel_id=1, replica_groups=mesh['px'=16,'py'=16] {'px','py'}, use_global_device_ids=true, to_apply=%region_6.0 | all-reduce | flops 1 | bytes 8 | tf_op jit(solution)/shard_map/psum | solution.py:103
  253.1 3.4 collective-permute-start.9
  260.2 4.1 collective-permute-done.8
  274.3 30.4 %psum.172 = f32[2]{0:T(128)S(1)} all-reduce(f32[2]{0:T(128)S(1)} %pad_maximum_fusion.92), channel_id=1, replica_groups=mesh['px'=16,'py'=16] {'px'}, use_global_device_ids=true, to_apply=%region_10.0 | all-reduce | flops 2 | bytes 16 | tf_op jit(solution)/shard_map/psum | solution.py:16
  304.8 20.0 %psum.173 = f32[2]{0:T(128)S(1)} all-reduce(f32[2]{0:T(128)S(1)} %psum.172), channel_id=1, replica_groups=mesh['px'=16,'py'=16] {'py'}, use_global_device_ids=true, to_apply=%region_11.0 | all-reduce | flops 2 | bytes 16 | tf_op jit(solution)/shard_map/psum | solution.py:16
  327.3 81.1 %psum.174 = f32[]{:T(128)} all-reduce(f32[]{:T(128)} %get-tuple-element.174), channel_id=1, replica_groups=mesh['px'=16,'py'=16] {'px','py'}, use_global_device_ids=true, to_apply=%region_13.0 | all-reduce | flops 1 | bytes 8 | tf_op jit(solution)/shard_map/psum | solution.py:103
  409.2 3.4 collective-permute-start.13
  415.2 5.3 collective-permute-done.12
  431.9 30.4 %psum.175 = f32[3]{0:T(128)S(1)} all-reduce(f32[3]{0:T(128)S(1)} %pad_maximum_fusion.93), channel_id=1, replica_groups=mesh['px'=16,'py'=16] {'px'}, use_global_device_ids=true, to_apply=%region_18.0 | all-reduce | flops 3 | bytes 24 | tf_op jit(solution)/shard_map/psum | solution.py:16
  462.3 20.0 %psum.176 = f32[3]{0:T(128)S(1)} all-reduce(f32[3]{0:T(128)S(1)} %psum.175), channel_id=1, replica_groups=mesh['px'=16,'py'=16] {'py'}, use_global_device_ids=true, to_apply=%region_19.0 | all-reduce | flops 3 | bytes 24 | tf_op jit(solution)/shard_map/psum | solution.py:16
  484.9 2.6 multiply_reduce_fusion.14
  489.0 81.1 %psum.177 = f32[]{:T(128)} all-reduce(f32[]{:T(128)} %multiply_reduce_fusion.14), channel_id=1, replica_groups=mesh['px'=16,'py'=16] {'px','py'}, use_global_device_ids=true, to_apply=%region_21.0 | all-reduce | flops 1 | bytes 8 | tf_op jit(solution)/shard_map/psum | solution.py:103
  584.3 73.4 %all-reduce.21 = (f32[8]{0:T(128)S(1)}, f32[8]{0:T(128)S(1)}) all-reduce(f32[8]{0:T(128)S(1)} %get-tuple-element.150, f32[8]{0:T(128)S(1)} %get-tuple-element.149), channel_id=1, replica_groups=mesh['px'=16,'py'=16] {'px','py'}, use_global_device_ids=true, to_apply=%region_28.30 | all-reduce | flops 16 | bytes 128 | tf_op jit(solution)/shard_map/psum | solution.py:88
  659.0 3.3 collective-permute-start.17
  662.3 2.5 collective-permute-start.16
  664.9 5.4 collective-permute-done.16
  674.8 3.0 collective-permute-done.19
  678.6 73.7 %psum.180 = f32[]{:T(128)} all-reduce(f32[]{:T(128)} %get-tuple-element.171), channel_id=1, replica_groups=mesh['px'=16,'py'=16] {'px','py'}, use_global_device_ids=true, to_apply=%region_31.0 | all-reduce | flops 1 | bytes 8 | tf_op jit(solution)/shard_map/psum | solution.py:88
  753.0 3.4 collective-permute-start.21
  758.9 5.4 collective-permute-done.20
  772.4 31.0 %psum.181 = f32[1]{0:T(128)} all-reduce(f32[1]{0:T(128)} %bitcast.32), channel_id=1, replica_groups=mesh['px'=16,'py'=16] {'px'}, use_global_device_ids=true, to_apply=%region_33.0 | all-reduce | flops 1 | bytes 8 | tf_op jit(solution)/shard_map/psum | solution.py:16
  803.3 20.2 %psum.182 = f32[1]{0:T(128)} all-reduce(f32[1]{0:T(128)} %psum.181), channel_id=1, replica_groups=mesh['px'=16,'py'=16] {'py'}, use_global_device_ids=true, to_apply=%region_34.0 | all-reduce | flops 1 | bytes 8 | tf_op jit(solution)/shard_map/psum | solution.py:16
  824.8 81.7 %psum.183 = f32[]{:T(128)} all-reduce(f32[]{:T(128)} %multiply_reduce_fusion.11), channel_id=1, replica_groups=mesh['px'=16,'py'=16] {'px','py'}, use_global_device_ids=true, to_apply=%region_36.0 | all-reduce | flops 1 | bytes 8 | tf_op jit(solution)/shard_map/psum | solution.py:103
  907.9 3.4 collective-permute-start.25
  913.8 5.4 collective-permute-done.24
  923.7 2.5 collective-permute-done.27
  929.2 30.4 %psum.184 = f32[2]{0:T(128)S(1)} all-reduce(f32[2]{0:T(128)S(1)} %pad_maximum_fusion.94), channel_id=1, replica_groups=mesh['px'=16,'py'=16] {'px'}, use_global_device_ids=true, to_apply=%region_39.0 | all-reduce | flops 2 | bytes 16 | tf_op jit(solution)/shard_map/psum | solution.py:16
  959.7 20.0 %psum.185 = f32[2]{0:T(128)S(1)} all-reduce(f32[2]{0:T(128)S(1)} %psum.184), channel_id=1, replica_groups=mesh['px'=16,'py'=16] {'py'}, use_global_device_ids=true, to_apply=%region_40.0 | all-reduce | flops 2 | bytes 16 | tf_op jit(solution)/shard_map/psum | solution.py:16
  982.2 81.1 %psum.186 = f32[]{:T(128)} all-reduce(f32[]{:T(128)} %get-tuple-element.166), channel_id=1, replica_groups=mesh['px'=16,'py'=16] {'px','py'}, use_global_device_ids=true, to_apply=%region_42.0 | all-reduce | flops 1 | bytes 8 | tf_op jit(solution)/shard_map/psum | solution.py:103
  1064.0 3.4 collective-permute-start.29
  1070.0 5.3 collective-permute-done.28
  1086.6 30.4 %psum.187 = f32[3]{0:T(128)S(1)} all-reduce(f32[3]{0:T(128)S(1)} %pad_maximum_fusion.95), channel_id=1, replica_groups=mesh['px'=16,'py'=16] {'px'}, use_global_device_ids=true, to_apply=%region_46.0 | all-reduce | flops 3 | bytes 24 | tf_op jit(solution)/shard_map/psum | solution.py:16
  1117.1 20.0 %psum.188 = f32[3]{0:T(128)S(1)} all-reduce(f32[3]{0:T(128)S(1)} %psum.187), channel_id=1, replica_groups=mesh['px'=16,'py'=16] {'py'}, use_global_device_ids=true, to_apply=%region_47.0 | all-reduce | flops 3 | bytes 24 | tf_op jit(solution)/shard_map/psum | solution.py:16
  1139.7 2.6 multiply_reduce_fusion.4
  1143.7 81.1 %psum.189 = f32[]{:T(128)} all-reduce(f32[]{:T(128)} %multiply_reduce_fusion.4), channel_id=1, replica_groups=mesh['px'=16,'py'=16] {'px','py'}, use_global_device_ids=true, to_apply=%region_49.0 | all-reduce | flops 1 | bytes 8 | tf_op jit(solution)/shard_map/psum | solution.py:103
  1239.0 73.4 %all-reduce.20 = (f32[8]{0:T(128)S(1)}, f32[8]{0:T(128)S(1)}) all-reduce(f32[8]{0:T(128)S(1)} %get-tuple-element.148, f32[8]{0:T(128)S(1)} %get-tuple-element.147), channel_id=1, replica_groups=mesh['px'=16,'py'=16] {'px','py'}, use_global_device_ids=true, to_apply=%region_54.0 | all-reduce | flops 16 | bytes 128 | tf_op jit(solution)/shard_map/psum | solution.py:88
  1313.8 3.3 collective-permute-start.33
  1317.1 2.5 collective-permute-start.32
  1319.7 5.4 collective-permute-done.32
  1329.6 3.0 collective-permute-done.35
  (165 shorter events, 120.7 us)
Async XLA Ops:
  0.6 103.3 %copy-start.3 = (s32[2]{0:T(128)S(1)}, s32[2]{0:T(128)}, u32[]{:S(2)}) copy-start(s32[2]{0:T(128)} %constant.311.clone.1) | copy-start | bytes 28
  0.6 19.2 %copy-start = (f32[8,16,512]{2,1,0:T(8,128)S(1)}, f32[8,16,512]{2,1,0:T(8,128)}, u32[]{:S(2)}) copy-start(f32[8,16,512]{2,1,0:T(8,128)} %param.27) | copy-start | bytes 786436
  1.5 5.8 collective-permute-start.1
  4.9 7.9 collective-permute-start
  12.8 5.5 collective-permute-start.2
  14.8 5.1 collective-permute-start.3
  98.1 6.5 collective-permute-start.5
  101.4 7.9 collective-permute-start.4
  109.4 4.5 collective-permute-start.6
  111.3 5.1 collective-permute-start.7
  253.1 7.2 collective-permute-start.9
  256.4 7.9 collective-permute-start.8
  264.4 4.5 collective-permute-start.10
  266.3 5.1 collective-permute-start.11
  409.2 6.0 collective-permute-start.13
  412.5 7.9 collective-permute-start.12
  420.5 6.3 collective-permute-start.14
  422.4 5.1 collective-permute-start.15
  427.5 156.1 %copy-start.1 = (f32[8,8,16,512]{3,2,1,0:T(8,128)S(1)}, f32[8,8,16,512]{3,2,1,0:T(8,128)}, u32[]{:S(2)}) copy-start(f32[8,8,16,512]{3,2,1,0:T(8,128)} %param.28) | copy-start | bytes 6291460
  659.0 5.9 collective-permute-start.17
  662.3 7.9 collective-permute-start.16
  670.3 4.5 collective-permute-start.18
  672.3 5.5 collective-permute-start.19
  753.0 5.9 collective-permute-start.21
  756.4 7.9 collective-permute-start.20
  764.3 4.7 collective-permute-start.22
  766.4 5.1 collective-permute-start.23
  907.9 5.9 collective-permute-start.25
  911.3 7.9 collective-permute-start.24
  919.2 4.5 collective-permute-start.26
  921.2 5.1 collective-permute-start.27
  1064.0 6.0 collective-permute-start.29
  1067.4 7.9 collective-permute-start.28
  1075.4 6.3 collective-permute-start.30
  1077.3 5.1 collective-permute-start.31
  1313.8 19.7 %copy-start.2 = (f32[8,16,512]{2,1,0:T(8,128)}, f32[8,16,512]{2,1,0:T(8,128)S(1)}, u32[]{:S(2)}) copy-start(f32[8,16,512]{2,1,0:T(8,128)S(1)} %multiply_add_fusion) | copy-start | bytes 786436
  1313.8 5.9 collective-permute-start.33
  1317.1 7.9 collective-permute-start.32
  1325.1 4.5 collective-permute-start.34
  1327.1 5.5 collective-permute-start.35
